TPU v7x, 32 devices: a whole 2x2x4 slice. The times are simulated.
32 devices in a mesh: freq: 16 (over z, y, core), chan: 2 (over x).
Axes of the slice: x: 2, y: 2, z: 4, core: 2. Of those that a mesh axis runs over, the one named last changes fastest.
Arguments:
- traces: bfloat16 [256, 2048, 256], P('freq', 'chan'), may hold values from -6 to 6
- channel_mask: int32 [2048], P('chan'), may hold values 0 or 1
- bin_index: int32 [16], replicated, may hold values from 1 to 127
Outputs:
- cross: bfloat16 [16, 2, 2048, 2048], P('freq', None, 'chan')
All inputs are finite; a program needn't handle non-finite values. No bound on the sum of `channel_mask` on one device may be relied on, other than what follows from the above.
Results may differ from a plain program's by a relative error of at most 0.0064.
Values may be sent and summed in bfloat16 or wider, within the bound.
No kernel may reach another device: no remote copies, remote signals or barrier semaphores. Data moves between devices by JAX's collectives and lax.ppermute only.
A program may use at most 64 MiB of HBM per device.

v0:
```python
import math
import jax
import jax.numpy as jnp
from jax import lax
from jax.sharding import PartitionSpec as P


def passed_along(value, axis, steps):
    count = lax.axis_size(axis)
    pairs = [(source, (source + steps) % count) for source in range(count)]
    return lax.ppermute(value, axis, pairs)


def shards(traces, channel_mask, bin_index):
    segment_local_rows, width, length = traces.shape
    nbins = bin_index.shape[0]
    samples = jnp.arange(length, dtype=jnp.int32)
    phase_index = bin_index[None, :] * samples[:, None] % length
    angles = 2.0 * math.pi / length * phase_index.astype(jnp.float32)
    wave_table = (
        jnp.stack([jnp.cos(angles), -jnp.sin(angles)], axis=2)
        .reshape(length, 2 * nbins)
        .astype(jnp.bfloat16)
    )
    taper_curve = 0.5 - 0.5 * jnp.cos(2.0 * math.pi / length * (samples.astype(jnp.float32) + 0.5))
    channel_gain = channel_mask.astype(jnp.float32)
    squares = jnp.einsum("sct,sct->sc", traces, traces, preferred_element_type=jnp.float32)
    spread = jnp.sqrt(squares / length + 1e-06)
    tapered = (
        traces.astype(jnp.float32)
        / spread[:, :, None]
        * taper_curve[None, None, :]
        * channel_gain[None, :, None]
    ).astype(jnp.bfloat16)
    segment_spectra = jnp.dot(
        tapered.reshape(segment_local_rows * width, length),
        wave_table,
        preferred_element_type=jnp.float32,
    )
    segment_spectra = segment_spectra.reshape(segment_local_rows, width, nbins, 2).transpose(
        2, 0, 3, 1
    )
    segment_spectra = lax.all_to_all(
        segment_spectra, "freq", split_axis=0, concat_axis=1, tiled=True
    )
    bins_local = segment_spectra.shape[0]
    segments = segment_spectra.shape[1]
    band_power = jnp.sum(segment_spectra * segment_spectra, axis=(1, 2)) / segments + 1e-06
    whitened = (segment_spectra / jnp.sqrt(band_power)[:, None, None, :]).astype(jnp.bfloat16)
    real_rows = whitened.reshape(bins_local, 2 * segments, width)
    turned = jnp.stack([whitened[:, :, 1], -whitened[:, :, 0]], axis=2).reshape(
        bins_local, 2 * segments, width
    )
    stacked_spectra = jnp.concatenate([real_rows, turned], axis=2)
    inverse = 1.0 / segments

    def block_cross_product(spectrum_fragment):
        cross_product_term = jnp.einsum(
            "mqr,mqe->mre", stacked_spectra, spectrum_fragment, preferred_element_type=jnp.float32
        )
        return (
            (cross_product_term * inverse)
            .reshape(bins_local, 2, width, spectrum_fragment.shape[2])
            .astype(jnp.bfloat16)
        )

    def place(result, spectrum_fragment, column):
        return lax.dynamic_update_slice(
            result, block_cross_product(spectrum_fragment), (0, 0, 0, column)
        )

    group = lax.axis_size("chan")
    own_index = lax.axis_index("chan")
    result = jnp.zeros((bins_local, 2, width, group * width), jnp.bfloat16)
    result = place(result, real_rows, own_index * width)
    moving = real_rows
    for step in range(1, group):
        moving = passed_along(moving, "chan", 1)
        result = place(result, moving, (own_index - step) % group * width)
    return result


def solution(mesh):
    in_specs = (P("freq", "chan", None), P("chan"), P())
    out_specs = P("freq", None, "chan", None)
    return jax.shard_map(shards, mesh=mesh, in_specs=in_specs, out_specs=out_specs, check_vma=False)
```

profile of v0, /device:TPU:14, one launch (start us, length us, event | category | flops | bytes accessed | tf_op | source)
XLA Modules:
  0.0 106.8 jit_solution(10640829522992178758)
XLA Ops:
  0.0 0.8 cosine_convert_fusion
  0.9 0.0 copy-start.3
  0.9 0.0 copy-start
  1.0 5.8 %fusion.3 = f32[16,1024]{1,0:T(8,128)S(1)} fusion(bf16[16,1024,256]{2,1,0:T(8,128)(2,1)} %param.3), kind=kLoop, calls=%fused_computation.5 | loop fusion | flops 12566528 | bytes 8454144 | tf_op jit(solution)/shard_map/sct,sct->sc/dot_general | solution.py:27
  6.8 0.0 copy-done.3
  6.8 0.0 copy-done
  6.8 3.3 %fusion.8 = f32[16,16,2,1024]{3,0,2,1:T(8,128)S(1)} fusion(bf16[16,1024,256]{2,1,0:T(8,128)(2,1)S(1)} %copy-done, f32[1024]{0:T(1024)S(1)} %convert_element_type.90, f32[256]{0:T(256)S(1)} %multiply_subtract_fusion, f32[16,1024]{1,0:T(8,128)S(1)} %add_sqrt_fusion, bf16[16,2,256]{2,1,0:T(2,128)(2,1)S(1)} %dot_general.18), kind=kOutput, calls=%fused_computation.16 | convolution fusion | flops 289406976 | bytes 10572800 | tf_op jit(solution)/shard_map/dot_general | solution.py:35
  10.1 2.9 %copy.15 = f32[16,16,2,1024]{3,2,1,0:T(2,128)} copy(f32[16,16,2,1024]{3,0,2,1:T(8,128)S(1)} %fusion.8) | data formatting | bytes 4194304 | tf_op jit(solution)/shard_map/transpose | solution.py:40
  13.0 6.2 %all-to-all-start = ((f32[16,16,2,1024]{3,2,1,0:T(2,128)}), f32[16,16,2,1024]{3,2,1,0:T(2,128)S(1)}, u32[]{:S(2)}, u32[]{:S(2)}) async-start(f32[16,16,2,1024]{3,2,1,0:T(2,128)} %copy.15), calls=%async_computation | async-start | bytes 4194304 | tf_op jit(solution)/shard_map/all_to_all | solution.py:43
  19.3 47.1 %all-to-all-done = f32[16,16,2,1024]{3,2,1,0:T(2,128)S(1)} async-done(((f32[16,16,2,1024]{3,2,1,0:T(2,128)}), f32[16,16,2,1024]{3,2,1,0:T(2,128)S(1)}, u32[]{:S(2)}, u32[]{:S(2)}) %all-to-all-start) | async-done | bytes 2097184 | tf_op jit(solution)/shard_map/all_to_all | solution.py:43
  66.4 0.9 multiply_reduce_fusion
  67.3 0.7 copy.16
  68.0 1.2 %fusion.7 = bf16[1,256,2,1024]{3,1,2,0:T(8,128)(2,1)} fusion(f32[16,16,2,1024]{3,1,0,2:T(8,128)S(1)} %copy.16, f32[1024]{0:T(1024)S(1)} %add_sqrt_fusion.1), kind=kLoop, calls=%fused_computation.12 | loop fusion | flops 1048576 | bytes 3149824 | tf_op jit(solution)/shard_map/convert_element_type | solution.py:49
  69.2 2.4 %all_to_all.12 = f32[1,512,1024]{2,1,0:T(8,128)} reshape(f32[16,16,2,1024]{3,2,1,0:T(2,128)S(1)} %all-to-all-done) | data formatting | bytes 4194304 | tf_op jit(solution)/shard_map/all_to_all | solution.py:43
  71.7 0.0 copy-start.2
  71.7 2.9 %divide_convert_fusion = bf16[1,512,1024]{2,1,0:T(8,128)(2,1)} fusion(f32[1,512,1024]{2,1,0:T(8,128)} %all_to_all.12, f32[1024]{0:T(1024)S(1)} %add_sqrt_fusion.1), kind=kLoop, calls=%fused_computation.13 | loop fusion | flops 1048576 | bytes 3149824 | tf_op jit(solution)/shard_map/convert_element_type | solution.py:49
  74.6 0.5 collective-permute-start
  75.1 0.9 divide_convert_fusion.1
  76.0 0.0 copy-done.2
  76.0 0.1 fusion.22
  76.1 0.1 pad_maximum_fusion
  76.2 1.1 %copy.17 = bf16[1,256,2,1024]{3,2,1,0:T(2,128)(2,1)S(1)} copy(bf16[1,256,2,1024]{3,1,2,0:T(8,128)(2,1)S(1)} %pad_maximum_fusion) | data formatting | bytes 2097152 | tf_op jit(solution)/shard_map/stack | solution.py:51
  77.3 0.4 reshape.233
  77.7 0.4 convert_element_type.97
  78.2 3.6 %multiply_convert_fusion.1 = bf16[2048,1024]{1,0:T(8,128)(2,1)S(1)} fusion(bf16[512,1024]{1,0:T(8,128)(2,1)S(1)} %convert_element_type.97, bf16[1,512,1024]{2,1,0:T(8,128)(2,1)S(1)} %reshape.233, bf16[1,512,1024]{2,1,0:T(8,128)(2,1)} %divide_convert_fusion), kind=kOutput, calls=%fused_computation.8 | convolution fusion | flops 2155872256 | bytes 7340032 | tf_op jit(solution)/shard_map/mqr,mqe->mre/dot_general | solution.py:58
  81.8 1.1 broadcast_in_dim.2
  82.9 0.6 constant_dynamic-update-slice_fusion.1
  83.5 0.0 copy-start.1
  83.5 16.9 %collective-permute-done = bf16[1,512,1024]{2,1,0:T(8,128)(2,1)} collective-permute-done((bf16[1,512,1024]{2,1,0:T(8,128)(2,1)}, bf16[1,512,1024]{2,1,0:T(8,128)(2,1)}, u32[]{:S(2)}, u32[]{:S(2)}) %collective-permute-start) | collective-permute-done | bytes 1048608 | tf_op jit(solution)/shard_map/ppermute | solution.py:11
  100.4 3.9 %multiply_convert_fusion = bf16[2048,1024]{1,0:T(8,128)(2,1)S(1)} fusion(bf16[1,512,1024]{2,1,0:T(8,128)(2,1)S(1)} %reshape.233, bf16[1,512,1024]{2,1,0:T(8,128)(2,1)} %divide_convert_fusion, bf16[1,512,1024]{2,1,0:T(8,128)(2,1)} %collective-permute-done), kind=kOutput, calls=%fused_computation.7 | convolution fusion | flops 2155872256 | bytes 7340032 | tf_op jit(solution)/shard_map/mqr,mqe->mre/dot_general | solution.py:58
  104.3 0.0 copy-done.1
  104.3 2.5 %constant_dynamic-update-slice_fusion = bf16[1,2,1024,2048]{3,2,1,0:T(8,128)(2,1)} fusion(bf16[1,2,1024,2048]{3,2,1,0:T(8,128)(2,1)} %copy-done.1, bf16[1,2,1024,1024]{3,2,1,0:T(8,128)(2,1)S(1)} %bitcast.29, s32[]{:T(128)S(6)} %select_n.33), kind=kLoop, calls=%fused_computation.37 | loop fusion | bytes 8388612 | tf_op jit(solution)/shard_map/dynamic_update_slice | solution.py:68
  (8 shorter events, 0.1 us)
Async XLA Ops:
  0.9 5.8 %copy-start.3 = (s32[1024]{0:T(1024)S(1)}, s32[1024]{0:T(1024)}, u32[]{:S(2)}) copy-start(s32[1024]{0:T(1024)} %param.4) | copy-start | bytes 12292
  0.9 5.8 %copy-start = (bf16[16,1024,256]{2,1,0:T(8,128)(2,1)S(1)}, bf16[16,1024,256]{2,1,0:T(8,128)(2,1)}, u32[]{:S(2)}) copy-start(bf16[16,1024,256]{2,1,0:T(8,128)(2,1)} %param.3) | copy-start | bytes 25165828
  13.0 53.4 %all-to-all-start = ((f32[16,16,2,1024]{3,2,1,0:T(2,128)}), f32[16,16,2,1024]{3,2,1,0:T(2,128)S(1)}, u32[]{:S(2)}, u32[]{:S(2)}) async-start(f32[16,16,2,1024]{3,2,1,0:T(2,128)} %copy.15), calls=%async_computation | async-start | bytes 4194304 | tf_op jit(solution)/shard_map/all_to_all | solution.py:43
  71.7 4.4 %copy-start.2 = (bf16[1,256,2,1024]{3,1,2,0:T(8,128)(2,1)S(1)}, bf16[1,256,2,1024]{3,1,2,0:T(8,128)(2,1)}, u32[]{:S(2)}) copy-start(bf16[1,256,2,1024]{3,1,2,0:T(8,128)(2,1)} %fusion.7) | copy-start | bytes 3145732
  74.6 25.8 %collective-permute-start = (bf16[1,512,1024]{2,1,0:T(8,128)(2,1)}, bf16[1,512,1024]{2,1,0:T(8,128)(2,1)}, u32[]{:S(2)}, u32[]{:S(2)}) collective-permute-start(bf16[1,512,1024]{2,1,0:T(8,128)(2,1)} %divide_convert_fusion), channel_id=1, source_target_pairs={{0,1},{1,0},{2,3},{3,2},{4,5},{5,4},{6,7},{7,6},{8,9},{9,8},{10,11... | collective-permute-start | bytes 3145736 | tf_op jit(solution)/shard_map/ppermute | solution.py:11
  83.5 20.8 %copy-start.1 = (bf16[1,2,1024,2048]{3,2,1,0:T(8,128)(2,1)}, bf16[1,2,1024,2048]{3,2,1,0:T(8,128)(2,1)S(1)}, u32[]{:S(2)}) copy-start(bf16[1,2,1024,2048]{3,2,1,0:T(8,128)(2,1)S(1)} %constant_dynamic-update-slice_fusion.1) | copy-start | bytes 25165828
where the time goes:
time: 107 us
  waiting for transfers between devices  64 us (60%)
  other arithmetic  12.8 us (12%)
  local copies, waits for them, and re-layouts  12.2 us (11%)
  matrix products  10.8 us (10%)
  starting transfers between devices  6.78 us (6%)
    all_to_all x1, waiting for transfers between devices, shards(): lax.all_to_all(segment_spectra, 'freq', split_axis=0, concat_axis=1, tile...  47.1 us
    ppermute x1, waiting for transfers between devices, passed_along(): return lax.ppermute(value, axis, pairs)  16.9 us
    dot_general x2, matrix products, block_cross_product(): jnp.einsum('mqr,mqe->mre', stacked_spectra, spectrum_fragment, preferred_...  7.53 us
    all_to_all x1, starting transfers between devices, shards(): lax.all_to_all(segment_spectra, 'freq', split_axis=0, concat_axis=1, tile...  6.24 us
    dot_general x1, other arithmetic, shards(): jnp.einsum('sct,sct->sc', traces, traces, preferred_element_type=jnp.floa...  5.77 us
    convert_element_type x3, other arithmetic, shards(): (segment_spectra / jnp.sqrt(band_power)[:, None, None, :]).astype(jnp.bfl...  5.04 us
    dot_general x1, matrix products, shards(): jnp.dot(tapered.reshape(segment_local_rows * width, length), wave_table,...  3.3 us
    all_to_all x2, local copies, waits for them, and re-layouts, shards(): lax.all_to_all(segment_spectra, 'freq', split_axis=0, concat_axis=1, tile...  3.09 us
  transfers between devices with their start and end apart: 2, of which 2 were waited for; matrix products, arithmetic and copies ran while one was open for 8% of the time, Pallas kernels for 0%

commit v1 on v0

--- a/solution.py
+++ b/solution.py
@@ -12,6 +12,14 @@
 
 
 def shards(traces, channel_mask, bin_index):
+
+    def things_link(x_in, ax_name="freq"):
+        placed = jnp.concatenate(
+            lax.all_to_all(jnp.stack(jnp.split(x_in, lax.psum(1, ax_name), axis=0)), ax_name, 0, 0),
+            axis=1,
+        )
+        return placed
+
     segment_local_rows, width, length = traces.shape
     nbins = bin_index.shape[0]
     samples = jnp.arange(length, dtype=jnp.int32)
@@ -40,9 +48,7 @@
     segment_spectra = segment_spectra.reshape(segment_local_rows, width, nbins, 2).transpose(
         2, 0, 3, 1
     )
-    segment_spectra = lax.all_to_all(
-        segment_spectra, "freq", split_axis=0, concat_axis=1, tiled=True
-    )
+    segment_spectra = things_link(segment_spectra)
     bins_local = segment_spectra.shape[0]
     segments = segment_spectra.shape[1]
     band_power = jnp.sum(segment_spectra * segment_spectra, axis=(1, 2)) / segments + 1e-06

time: 107 us -> 134 us (1.25)
  local copies, waits for them, and re-layouts: 12.2 us -> 27.1 us
  other arithmetic: 12.8 us -> 22.5 us
  matrix products: 10.8 us -> 14.3 us
    another operation x0 -> x3, local copies, waits for them, and re-layouts: none -> 9.91 us  [things_link(): jnp.stack(jnp.split(x_in, lax.psum(1, ax_name), axis=0))]
    concatenate x0 -> x1, other arithmetic: none -> 8.59 us  [shards(): stacked_spectra = jnp.concatenate([real_rows, turned], axis=2)]
    reshape x0 -> x1, local copies, waits for them, and re-layouts: none -> 4.24 us  [things_link(): jnp.concatenate(lax.all_to_all(jnp.stack(jnp.split(x_in, lax.psum(1, ax_n...]
    dot_general x2, matrix products: 7.53 us -> 11 us  [block_cross_product(): jnp.einsum('mqr,mqe->mre', stacked_spectra, spectrum_fragment, preferred_...]
    convert_element_type x1 -> x2, local copies, waits for them, and re-layouts: 0.44 us -> 3.67 us  [shards(): (segment_spectra / jnp.sqrt(band_power)[:, None, None, :]).astype(jnp.bfl...]
    transpose x1 -> x0, local copies, waits for them, and re-layouts: 2.94 us -> none  [shards(): segment_spectra.reshape(segment_local_rows, width, nbins, 2)]
    reshape x1, local copies, waits for them, and re-layouts: 0.44 us -> 3.33 us  [shards(): jnp.stack([whitened[:, :, 1], -whitened[:, :, 0]], axis=2)]
    all_to_all x2 -> x1, local copies, waits for them, and re-layouts: 3.09 us -> 0.68 us  [things_link(): lax.all_to_all(jnp.stack(jnp.split(x_in, lax.psum(1, ax_name), axis=0)),...]
  transfers between devices with their start and end apart: 2 -> 2, of which waited for: 2 -> 2; matrix products, arithmetic and copies ran while one was open for 8% -> 7% of each run, Pallas kernels for 0% -> 0%
where the time goes in v1:
time: 134 us
  waiting for transfers between devices  63.1 us (47%)
  local copies, waits for them, and re-layouts  27.1 us (20%)
  other arithmetic  22.5 us (17%)
  matrix products  14.3 us (11%)
  starting transfers between devices  6.78 us (5%)
    all_to_all x1, waiting for transfers between devices, things_link(): lax.all_to_all(jnp.stack(jnp.split(x_in, lax.psum(1, ax_name), axis=0)),...  47.1 us
    ppermute x1, waiting for transfers between devices, passed_along(): return lax.ppermute(value, axis, pairs)  15.9 us
    dot_general x2, matrix products, block_cross_product(): jnp.einsum('mqr,mqe->mre', stacked_spectra, spectrum_fragment, preferred_...  11 us
    another operation x3, local copies, waits for them, and re-layouts, things_link(): jnp.stack(jnp.split(x_in, lax.psum(1, ax_name), axis=0))  9.91 us
    concatenate x1, other arithmetic, shards(): stacked_spectra = jnp.concatenate([real_rows, turned], axis=2)  8.59 us
    all_to_all x1, starting transfers between devices, things_link(): lax.all_to_all(jnp.stack(jnp.split(x_in, lax.psum(1, ax_name), axis=0)),...  6.24 us
    dot_general x1, other arithmetic, shards(): jnp.einsum('sct,sct->sc', traces, traces, preferred_element_type=jnp.floa...  5.77 us
    convert_element_type x3, other arithmetic, shards(): (segment_spectra / jnp.sqrt(band_power)[:, None, None, :]).astype(jnp.bfl...  5.46 us
  transfers between devices with their start and end apart: 2, of which 2 were waited for; matrix products, arithmetic and copies ran while one was open for 7% of the time, Pallas kernels for 0%

profile of v1, /device:TPU:14, one launch (start us, length us, event | category | flops | bytes accessed | tf_op | source)
XLA Modules:
  0.0 133.8 jit_solution(11098134617697180132)
XLA Ops:
  0.0 0.7 convert_element_type.90
  0.7 0.8 cosine_convert_fusion
  1.6 0.0 copy-start
  1.6 5.8 %fusion.3 = f32[16,1024]{1,0:T(8,128)S(1)} fusion(bf16[16,1024,256]{2,1,0:T(8,128)(2,1)} %param.3), kind=kLoop, calls=%fused_computation.5 | loop fusion | flops 12566528 | bytes 8454144 | tf_op jit(solution)/shard_map/sct,sct->sc/dot_general | solution.py:35
  7.4 0.0 copy-done
  7.4 3.3 %fusion.10 = f32[16,16,2,1024]{3,0,2,1:T(8,128)S(1)} fusion(bf16[16,1024,256]{2,1,0:T(8,128)(2,1)S(1)} %copy-done, f32[1024]{0:T(1024)S(1)} %convert_element_type.90, f32[256]{0:T(256)S(1)} %multiply_subtract_fusion, f32[16,1024]{1,0:T(8,128)S(1)} %add_sqrt_fusion, bf16[16,2,256]{2,1,0:T(2,128)(2,1)S(1)} %dot_general.18), kind=kOutput, calls=%fused_computation.18 | convolution fusion | flops 289406976 | bytes 10572800 | tf_op jit(solution)/shard_map/dot_general | solution.py:43
  10.7 2.5 %slice_bitcast_fusion = (f32[1,1,16,2,1024]{4,0,3,2,1:T(1,128)S(1)}, f32[1,1,16,2,1024]{4,0,3,2,1:T(1,128)S(1)}, f32[1,1,16,2,1024]{4,0,3,2,1:T(1,128)S(1)}, f32...) fusion(f32[16,16,2,1024]{3,0,2,1:T(8,128)S(1)} %fusion.10), kind=kLoop, calls=%fused_computation.24 | loop fusion | bytes 4194304 | tf_op jit(solution)/shard_map/stack | solution.py:18
  13.3 4.4 %stack.78 = f32[16,1,16,2,1024]{4,0,3,2,1:T(8,128)S(1)} concatenate(f32[1,1,16,2,1024]{4,0,3,2,1:T(1,128)} %get-tuple-element.20, f32[1,1,16,2,1024]{4,0,3,2,1:T(1,128)} %get-tuple-element.19, f32[1,1,16,2,1024]{4,0,3,2,1:T(1,128)} %get-tuple-element.18, f32[1,1,16,2,1024]{4,0,3,2,1:T(1,128)} %get-tuple-element.17, f32[1,1,16,2,1024]{4,0,3,2,1:T(1,128)} %get-tuple-element.16, ...), dimensions={0} | concatenate | bytes 4194304 | tf_op jit(solution)/shard_map/stack | solution.py:18
  17.7 2.9 %copy.23 = f32[16,1,16,2,1024]{4,3,2,1,0:T(2,128)} copy(f32[16,1,16,2,1024]{4,0,3,2,1:T(8,128)S(1)} %stack.78) | data formatting | bytes 4194304 | tf_op jit(solution)/shard_map/stack | solution.py:18
  20.7 6.2 %all-to-all-start = ((f32[16,1,16,2,1024]{4,3,2,1,0:T(2,128)}), f32[16,1,16,2,1024]{4,3,2,1,0:T(2,128)S(1)}, u32[]{:S(2)}, u32[]{:S(2)}) async-start(f32[16,1,16,2,1024]{4,3,2,1,0:T(2,128)} %copy.23), calls=%async_computation | async-start | bytes 4194304 | tf_op jit(solution)/shard_map/all_to_all | solution.py:18
  26.9 47.1 %all-to-all-done = f32[16,1,16,2,1024]{4,3,2,1,0:T(2,128)S(1)} async-done(((f32[16,1,16,2,1024]{4,3,2,1,0:T(2,128)}), f32[16,1,16,2,1024]{4,3,2,1,0:T(2,128)S(1)}, u32[]{:S(2)}, u32[]{:S(2)}) %all-to-all-start) | async-done | bytes 2097184 | tf_op jit(solution)/shard_map/all_to_all | solution.py:18
  74.0 0.9 multiply_reduce_fusion
  74.9 0.7 copy.24
  75.6 0.3 fusion.9
  75.9 4.2 %reshape.235 = f32[1,512,1024]{2,0,1:T(1,128)} reshape(f32[16,1,16,2,1024]{4,3,2,1,0:T(2,128)S(1)} %all-to-all-done) | data formatting | bytes 4194304 | tf_op jit(solution)/shard_map/reshape | solution.py:17
  80.1 4.3 %divide_convert_fusion = bf16[1,512,1024]{2,0,1:T(2,128)(2,1)} fusion(f32[1,512,1024]{2,0,1:T(1,128)} %reshape.235, f32[1024]{0:T(1024)S(1)} %add_sqrt_fusion.1), kind=kLoop, calls=%fused_computation.15 | loop fusion | flops 1048576 | bytes 3149824 | tf_op jit(solution)/shard_map/convert_element_type | solution.py:55
  84.5 0.1 fusion.24
  84.6 0.1 pad_maximum_fusion.1
  84.7 1.1 copy.25
  85.7 3.3 %reshape.244 = bf16[1,512,1024]{2,0,1:T(2,128)(2,1)} reshape(bf16[1,256,2,1024]{3,2,1,0:T(2,128)(2,1)S(1)} %copy.25) | data formatting | bytes 2097152 | tf_op jit(solution)/shard_map/reshape | solution.py:57
  89.1 3.0 %copy.27 = bf16[1,512,1024]{2,1,0:T(8,128)(2,1)} copy(bf16[1,512,1024]{2,0,1:T(2,128)(2,1)} %divide_convert_fusion) | data formatting | bytes 2097152 | tf_op jit(solution)/shard_map/convert_element_type | solution.py:55
  92.0 8.6 %pad_maximum_fusion = bf16[1,512,2048]{2,0,1:T(2,128)(2,1)} fusion(bf16[1,512,1024]{2,0,1:T(2,128)(2,1)} %reshape.244, bf16[1,512,1024]{2,0,1:T(2,128)(2,1)} %divide_convert_fusion), kind=kLoop, calls=%fused_computation.10 | loop fusion | flops 4194304 | bytes 4194304 | tf_op jit(solution)/shard_map/concatenate | solution.py:60
  100.6 0.5 collective-permute-start
  101.2 0.9 divide_convert_fusion.1
  102.0 0.7 convert_element_type.97
  102.7 6.0 %multiply_convert_fusion.1 = bf16[2048,1024]{1,0:T(8,128)(2,1)S(1)} fusion(bf16[512,1024]{1,0:T(8,128)(2,1)S(1)} %convert_element_type.97, bf16[1,512,2048]{2,0,1:T(2,128)(2,1)} %pad_maximum_fusion), kind=kOutput, calls=%fused_computation.8 | convolution fusion | flops 2151677952 | bytes 7340032 | tf_op jit(solution)/shard_map/mqr,mqe->mre/dot_general | solution.py:64
  108.8 1.1 broadcast_in_dim.2
  109.8 0.0 copy-start.2
  109.8 0.6 constant_dynamic-update-slice_fusion.1
  110.5 0.0 copy-start.1
  110.5 15.9 %collective-permute-done = bf16[1,512,1024]{2,1,0:T(8,128)(2,1)} collective-permute-done((bf16[1,512,1024]{2,1,0:T(8,128)(2,1)}, bf16[1,512,1024]{2,1,0:T(8,128)(2,1)}, u32[]{:S(2)}, u32[]{:S(2)}) %collective-permute-start) | collective-permute-done | bytes 1048608 | tf_op jit(solution)/shard_map/ppermute | solution.py:11
  126.4 0.0 copy-done.2
  126.4 5.0 %multiply_convert_fusion = bf16[2048,1024]{1,0:T(8,128)(2,1)S(1)} fusion(bf16[1,512,1024]{2,1,0:T(8,128)(2,1)} %collective-permute-done, bf16[1,512,2048]{2,0,1:T(2,128)(2,1)S(1)} %copy-done.2), kind=kOutput, calls=%fused_computation.7 | convolution fusion | flops 2151677952 | bytes 7340032 | tf_op jit(solution)/shard_map/mqr,mqe->mre/dot_general | solution.py:64
  131.4 0.0 copy-done.1
  131.4 2.5 %constant_dynamic-update-slice_fusion = bf16[1,2,1024,2048]{3,2,1,0:T(8,128)(2,1)} fusion(bf16[1,2,1024,2048]{3,2,1,0:T(8,128)(2,1)} %copy-done.1, bf16[1,2,1024,1024]{3,2,1,0:T(8,128)(2,1)S(1)} %bitcast.63, s32[]{:T(128)S(6)} %select_n.33), kind=kLoop, calls=%fused_computation.57 | loop fusion | bytes 8388612 | tf_op jit(solution)/shard_map/dynamic_update_slice | solution.py:74
  (7 shorter events, 0.1 us)
Async XLA Ops:
  1.6 5.8 %copy-start = (bf16[16,1024,256]{2,1,0:T(8,128)(2,1)S(1)}, bf16[16,1024,256]{2,1,0:T(8,128)(2,1)}, u32[]{:S(2)}) copy-start(bf16[16,1024,256]{2,1,0:T(8,128)(2,1)} %param.3) | copy-start | bytes 25165828
  20.7 53.4 %all-to-all-start = ((f32[16,1,16,2,1024]{4,3,2,1,0:T(2,128)}), f32[16,1,16,2,1024]{4,3,2,1,0:T(2,128)S(1)}, u32[]{:S(2)}, u32[]{:S(2)}) async-start(f32[16,1,16,2,1024]{4,3,2,1,0:T(2,128)} %copy.23), calls=%async_computation | async-start | bytes 4194304 | tf_op jit(solution)/shard_map/all_to_all | solution.py:18
  100.6 25.8 %collective-permute-start = (bf16[1,512,1024]{2,1,0:T(8,128)(2,1)}, bf16[1,512,1024]{2,1,0:T(8,128)(2,1)}, u32[]{:S(2)}, u32[]{:S(2)}) collective-permute-start(bf16[1,512,1024]{2,1,0:T(8,128)(2,1)} %copy.27), channel_id=1, source_target_pairs={{0,1},{1,0},{2,3},{3,2},{4,5},{5,4},{6,7},{7,6},{8,9},{9,8},{10,11... | collective-permute-start | bytes 3145736 | tf_op jit(solution)/shard_map/ppermute | solution.py:11
  109.8 16.6 %copy-start.2 = (bf16[1,512,2048]{2,0,1:T(2,128)(2,1)S(1)}, bf16[1,512,2048]{2,0,1:T(2,128)(2,1)}, u32[]{:S(2)}) copy-start(bf16[1,512,2048]{2,0,1:T(2,128)(2,1)} %pad_maximum_fusion) | copy-start | bytes 6291460
  110.5 20.9 %copy-start.1 = (bf16[1,2,1024,2048]{3,2,1,0:T(8,128)(2,1)}, bf16[1,2,1024,2048]{3,2,1,0:T(8,128)(2,1)S(1)}, u32[]{:S(2)}) copy-start(bf16[1,2,1024,2048]{3,2,1,0:T(8,128)(2,1)S(1)} %constant_dynamic-update-slice_fusion.1) | copy-start | bytes 25165828
